TPU v7x, 32 devices: a whole 2x2x4 slice. The times are simulated.
32 devices in a mesh: dp: 8 (over y, x, core), mp: 4 (over z).
Axes of the slice: x: 2, y: 2, z: 4, core: 2. Of those that a mesh axis runs over, the one named last changes fastest.
Arguments:
- tokens: bfloat16 [17408, 1024], P(('dp', 'mp')), may hold values from -6 to 6
- groups: int32 [17408], P(('dp', 'mp')), may hold values from 0 to 15
- lengths: int32 [16], P('dp'), may hold values from 272 to 1088, as said below
- qkv_weight: bfloat16 [3, 1024, 1024], P(None, None, 'mp'), may hold values from -0.1875 to 0.1875
- qv_bias: bfloat16 [2, 1024], P(None, 'mp'), may hold values from -3 to 3
- out_weight: bfloat16 [1024, 1024], P('mp'), may hold values from -1.5 to 1.5
- out_bias: bfloat16 [1024], replicated, may hold values from -2 to 2
- up_weight: bfloat16 [1024, 4096], P(None, 'mp'), may hold values from -0.1875 to 0.1875
- up_bias: bfloat16 [4096], P('mp'), may hold values from -3 to 3
- down_weight: bfloat16 [4096, 1024], P('mp'), may hold values from -0.09375 to 0.09375
- down_bias: bfloat16 [1024], replicated, may hold values from -2 to 2
- norm_gain: bfloat16 [4, 1024], replicated, may hold values from 0.5 to 1.5
- norm_bias: bfloat16 [4, 1024], replicated, may hold values from -2 to 2
- group_table: bfloat16 [16, 1024], replicated, may hold values from -3 to 3
- cotangent: bfloat16 [17408, 1024], P(('dp', 'mp')), may hold values from -6 to 6
Outputs:
- output: bfloat16 [17408, 1024], P(('dp', 'mp'))
- input_grad: float32 [17408, 1024], P(('dp', 'mp'))
- qkv_grad: float32 [3, 1024, 1024], P(None, None, 'mp')
- qv_bias_grad: float32 [2, 1024], P(None, 'mp')
- out_weight_grad: float32 [1024, 1024], P('mp')
- out_bias_grad: float32 [1024], replicated
- up_weight_grad: float32 [1024, 4096], P(None, 'mp')
- up_bias_grad: float32 [4096], P('mp')
- down_weight_grad: float32 [4096, 1024], P('mp')
- down_bias_grad: float32 [1024], replicated
- norm_gain_grad: float32 [4, 1024], replicated
- norm_bias_grad: float32 [4, 1024], replicated
- group_table_grad: float32 [16, 1024], replicated
Inputs may be any that keep to these rules, and one draw needn't show every extreme that they name: `lengths`: each sequence's valid length; some sequence has all 1088 tokens valid and some only 272.
All inputs are finite; a program needn't handle non-finite values.
Results may differ from a plain program's by a relative error of at most 0.009.
Values may be sent and summed in bfloat16 or wider, within the bound.
No kernel may reach another device: no remote copies, remote signals or barrier semaphores. Data moves between devices by JAX's collectives and lax.ppermute only.
A program may use at most 192 MiB of HBM per device.

v0:
```python
import math
import jax
import jax.numpy as jnp
from jax import lax
from jax.sharding import PartitionSpec as P

HEAD_DIM = 64
SEQ_LEN = 1088
RELAX_ALPHA = 32.0
NORM_EPSILON = 1e-05
MASKED_SCORE = -1000000000.0
PRECISE = lax.Precision.HIGHEST


def norm_forward(inputs, gain_row, shift_row):
    centred = inputs - jnp.mean(inputs, axis=-1, keepdims=True)
    factor = lax.rsqrt(jnp.mean(centred * centred, axis=-1, keepdims=True) + NORM_EPSILON)
    normal = centred * factor
    return (normal * gain_row + shift_row, normal, factor)


def norm_backward(upstream, normal, factor, gain_row):
    scaled = upstream * gain_row
    adjusted = (
        scaled
        - jnp.mean(scaled, axis=-1, keepdims=True)
        - normal * jnp.mean(scaled * normal, axis=-1, keepdims=True)
    )
    return (adjusted * factor, jnp.sum(upstream * normal, axis=0), jnp.sum(upstream, axis=0))


def block_mask(block_index, block_rows, key_reach, length):
    row_ids = block_index * block_rows + lax.broadcasted_iota(jnp.int32, (block_rows, key_reach), 0)
    columns = lax.broadcasted_iota(jnp.int32, (block_rows, key_reach), 1)
    return (columns <= row_ids) & (columns < length)


def block_scores(queries, keys_seq, block_index, block_rows, length):
    key_reach = (block_index + 1) * block_rows
    first = block_index * block_rows
    scores = jnp.einsum(
        "qhd,khd->hqk",
        queries[first:key_reach],
        keys_seq[:key_reach],
        preferred_element_type=jnp.float32,
    )
    visible = block_mask(block_index, block_rows, key_reach, length)[None]
    return (jnp.where(visible, scores, MASKED_SCORE), visible)


def attend(inputs):
    queries, keys_seq, values_seq, length = inputs
    block_rows = queries.shape[0] // 2
    pieces = []
    log_sums = []
    for block_index in range(2):
        key_reach = (block_index + 1) * block_rows
        scores, visible = block_scores(queries, keys_seq, block_index, block_rows, length)
        row_top = jnp.max(scores, axis=-1, keepdims=True)
        exponent = jnp.exp((scores - row_top) * RELAX_ALPHA)
        row_total = jnp.sum(exponent, axis=-1, keepdims=True)
        probs_low = (exponent / row_total).astype(jnp.bfloat16)
        pieces.append(
            jnp.einsum(
                "hqk,khd->qhd",
                probs_low,
                values_seq[:key_reach],
                preferred_element_type=jnp.float32,
            )
        )
        log_sums.append((row_top * RELAX_ALPHA + jnp.log(row_total))[..., 0])
    return (jnp.concatenate(pieces, axis=0), jnp.concatenate(log_sums, axis=1))


def attend_back(inputs):
    queries, keys_seq, values_seq, length, log_sums, grad_out = inputs
    block_rows = queries.shape[0] // 2
    grad_keys = jnp.zeros(keys_seq.shape, jnp.float32)
    grad_values = jnp.zeros(values_seq.shape, jnp.float32)
    grad_pieces = []
    for block_index in range(2):
        key_reach = (block_index + 1) * block_rows
        first = block_index * block_rows
        scores, visible = block_scores(queries, keys_seq, block_index, block_rows, length)
        exact = jnp.where(
            visible, jnp.exp(scores * RELAX_ALPHA - log_sums[:, first:key_reach, None]), 0.0
        )
        grad_rows = grad_out[first:key_reach]
        grad_probs = jnp.einsum(
            "qhd,khd->hqk", grad_rows, values_seq[:key_reach], preferred_element_type=jnp.float32
        )
        grad_values = grad_values.at[:key_reach].add(
            jnp.einsum(
                "hqk,qhd->khd",
                exact.astype(jnp.bfloat16),
                grad_rows,
                preferred_element_type=jnp.float32,
            )
        )
        row_delta = jnp.sum(exact * grad_probs, axis=-1, keepdims=True)
        grad_scores = (exact * (grad_probs - row_delta) * RELAX_ALPHA).astype(jnp.bfloat16)
        grad_pieces.append(
            jnp.einsum(
                "hqk,khd->qhd",
                grad_scores,
                keys_seq[:key_reach],
                preferred_element_type=jnp.float32,
            )
        )
        grad_keys = grad_keys.at[:key_reach].add(
            jnp.einsum(
                "hqk,qhd->khd",
                grad_scores,
                queries[first:key_reach],
                preferred_element_type=jnp.float32,
            )
        )
    return (jnp.concatenate(grad_pieces, axis=0), grad_keys, grad_values)


def on_device(
    tokens,
    groups,
    lengths,
    qkv_weight,
    qv_bias,
    out_weight,
    out_bias,
    up_weight,
    up_bias,
    down_weight,
    down_bias,
    norm_gain,
    norm_bias,
    group_table,
    cotangent,
):
    gains = norm_gain.astype(jnp.float32)
    shifts = norm_bias.astype(jnp.float32)
    row_count = tokens.shape[0]
    onehot = (
        groups[:, None] == lax.broadcasted_iota(jnp.int32, (1, group_table.shape[0]), 1)
    ).astype(jnp.bfloat16)
    residual = tokens.astype(jnp.float32) + jnp.dot(
        onehot, group_table, preferred_element_type=jnp.float32
    )
    normed, norm_one, inv_one = norm_forward(residual, gains[0], shifts[0])
    normed_low = normed.astype(jnp.bfloat16)
    normed_all = lax.all_gather(normed_low, "mp", axis=0, tiled=True)
    projected = jnp.einsum(
        "td,cde->cte", normed_all, qkv_weight, preferred_element_type=jnp.float32
    )
    local_width = qkv_weight.shape[2]
    seq_count = lengths.shape[0]
    head_shape = (seq_count, SEQ_LEN, local_width // HEAD_DIM, HEAD_DIM)
    factor = 1.0 / (RELAX_ALPHA * math.sqrt(HEAD_DIM))
    biases = qv_bias.astype(jnp.float32)
    queries = ((projected[0] + biases[0]) * factor).astype(jnp.bfloat16).reshape(head_shape)
    keys_all = projected[1].astype(jnp.bfloat16).reshape(head_shape)
    values_all = (projected[2] + biases[1]).astype(jnp.bfloat16).reshape(head_shape)
    attended, log_sums = lax.map(attend, (queries, keys_all, values_all, lengths))
    attended_low = attended.reshape(seq_count * SEQ_LEN, local_width).astype(jnp.bfloat16)
    branch = lax.psum_scatter(
        jnp.dot(
            lax.slice_in_dim(attended_low, 0, row_count * lax.axis_size("mp"), axis=0),
            out_weight,
            preferred_element_type=jnp.float32,
        ),
        "mp",
        scatter_dimension=0,
        tiled=True,
    ) + out_bias.astype(jnp.float32)
    branch_out, norm_two, inv_two = norm_forward(branch, gains[1], shifts[1])
    middle = residual + branch_out
    mid_normed, norm_three, inv_three = norm_forward(middle, gains[2], shifts[2])
    mid_low = mid_normed.astype(jnp.bfloat16)
    mid_all = lax.all_gather(mid_low, "mp", axis=0, tiled=True)
    pre_act = jnp.dot(mid_all, up_weight, preferred_element_type=jnp.float32) + up_bias.astype(
        jnp.float32
    )
    activated, gelu_pull = jax.vjp(jax.nn.gelu, pre_act)
    activated_low = activated.astype(jnp.bfloat16)
    ffn_out = lax.psum_scatter(
        jnp.dot(
            lax.slice_in_dim(activated_low, 0, row_count * lax.axis_size("mp"), axis=0),
            down_weight,
            preferred_element_type=jnp.float32,
        ),
        "mp",
        scatter_dimension=0,
        tiled=True,
    ) + down_bias.astype(jnp.float32)
    ffn_normed, norm_four, inv_four = norm_forward(ffn_out, gains[3], shifts[3])
    output = (middle + ffn_normed).astype(jnp.bfloat16)
    upstream = cotangent.astype(jnp.float32)
    grad_ffn, gain_four, shift_four = norm_backward(upstream, norm_four, inv_four, gains[3])
    grad_ffn_low = grad_ffn.astype(jnp.bfloat16)
    down_bias_part = jnp.sum(grad_ffn_low.astype(jnp.float32), axis=0)
    grad_ffn_all = lax.all_gather(grad_ffn_low, "mp", axis=0, tiled=True)
    down_grad = jnp.dot(activated_low.T, grad_ffn_all, preferred_element_type=jnp.float32)
    grad_act = jnp.dot(grad_ffn_all, down_weight.T, preferred_element_type=jnp.float32)
    (grad_pre,) = gelu_pull(grad_act)
    grad_pre_low = grad_pre.astype(jnp.bfloat16)
    up_bias_grad = jnp.sum(grad_pre_low.astype(jnp.float32), axis=0)
    up_grad = jnp.dot(mid_all.T, grad_pre_low, preferred_element_type=jnp.float32)
    grad_mid = lax.psum_scatter(
        jnp.dot(
            lax.slice_in_dim(grad_pre_low, 0, row_count * lax.axis_size("mp"), axis=0),
            up_weight.T,
            preferred_element_type=jnp.float32,
        ),
        "mp",
        scatter_dimension=0,
        tiled=True,
    )
    back_three, gain_three, shift_three = norm_backward(grad_mid, norm_three, inv_three, gains[2])
    grad_middle = upstream + back_three
    grad_branch, gain_two, shift_two = norm_backward(grad_middle, norm_two, inv_two, gains[1])
    grad_branch_low = grad_branch.astype(jnp.bfloat16)
    out_bias_part = jnp.sum(grad_branch_low.astype(jnp.float32), axis=0)
    grad_branch_all = lax.all_gather(grad_branch_low, "mp", axis=0, tiled=True)
    out_grad = jnp.dot(attended_low.T, grad_branch_all, preferred_element_type=jnp.float32)
    grad_attended = (
        jnp.dot(grad_branch_all, out_weight.T, preferred_element_type=jnp.float32)
        .astype(jnp.bfloat16)
        .reshape(head_shape)
    )
    grad_queries, grad_keys, grad_values = lax.map(
        attend_back, (queries, keys_all, values_all, lengths, log_sums, grad_attended)
    )
    flat_shape = (seq_count * SEQ_LEN, local_width)
    grad_q_low = (grad_queries * factor).astype(jnp.bfloat16).reshape(flat_shape)
    grad_k_low = grad_keys.astype(jnp.bfloat16).reshape(flat_shape)
    grad_v_low = grad_values.astype(jnp.bfloat16).reshape(flat_shape)
    grad_projected = jnp.stack([grad_q_low, grad_k_low, grad_v_low])
    qv_bias_grad = jnp.stack(
        [
            jnp.sum(grad_q_low.astype(jnp.float32), axis=0),
            jnp.sum(grad_v_low.astype(jnp.float32), axis=0),
        ]
    )
    qkv_grad = jnp.einsum(
        "td,cte->cde", normed_all, grad_projected, preferred_element_type=jnp.float32
    )
    grad_normed = lax.psum_scatter(
        jnp.einsum(
            "cte,cde->td",
            lax.slice_in_dim(grad_projected, 0, row_count * lax.axis_size("mp"), axis=1),
            qkv_weight,
            preferred_element_type=jnp.float32,
        ).astype(jnp.bfloat16),
        "mp",
        scatter_dimension=0,
        tiled=True,
    ).astype(jnp.float32)
    back_one, gain_one, shift_one = norm_backward(grad_normed, norm_one, inv_one, gains[0])
    input_grad = grad_middle + back_one
    table_part = jnp.dot(
        onehot.astype(jnp.float32).T,
        input_grad,
        precision=PRECISE,
        preferred_element_type=jnp.float32,
    )
    gain_parts = jnp.stack([gain_one, gain_two, gain_three, gain_four])
    shift_parts = jnp.stack([shift_one, shift_two, shift_three, shift_four])
    qkv_grad, qv_bias_grad, out_grad, up_grad, up_bias_grad, down_grad = lax.psum(
        (qkv_grad, qv_bias_grad, out_grad, up_grad, up_bias_grad, down_grad), "dp"
    )
    gain_grad, shift_grad, out_bias_grad, down_bias_grad, table_grad = lax.psum(
        (gain_parts, shift_parts, out_bias_part, down_bias_part, table_part), ("dp", "mp")
    )
    return (
        output,
        input_grad,
        qkv_grad,
        qv_bias_grad,
        out_grad,
        out_bias_grad,
        up_grad,
        up_bias_grad,
        down_grad,
        down_bias_grad,
        gain_grad,
        shift_grad,
        table_grad,
    )


def solution(mesh):
    placed = (
        P(("dp", "mp"), None),
        P(("dp", "mp")),
        P("dp"),
        P(None, None, "mp"),
        P(None, "mp"),
        P("mp", None),
        P(),
        P(None, "mp"),
        P("mp"),
        P("mp", None),
        P(),
        P(),
        P(),
        P(),
        P(("dp", "mp"), None),
    )
    return jax.shard_map(
        on_device,
        mesh=mesh,
        in_specs=placed,
        out_specs=(
            P(("dp", "mp"), None),
            P(("dp", "mp"), None),
            P(None, None, "mp"),
            P(None, "mp"),
            P("mp", None),
            P(),
            P(None, "mp"),
            P("mp"),
            P("mp", None),
            P(),
            P(),
            P(),
            P(),
        ),
        check_vma=False,
    )
```

profile of v0, /device:TPU:1, one launch (start us, length us, event | category | flops | bytes accessed | tf_op | source)
XLA Modules:
  0.0 1619.4 jit_solution(17449451052311089601)
XLA Ops:
  15.2 87.1 %all-gather.5.cloned.1.call-done = bf16[2176,1024]{1,0:T(8,128)(2,1)} async-done(((bf16[544,1024]{1,0:T(8,128)(2,1)}), bf16[2176,1024]{1,0:T(8,128)(2,1)}) %all-gather.5.cloned.1.call-update) | async-done | bytes 4456464 | tf_op jit(solution)/shard_map/all_gather | solution.py:149
  102.3 5.9 convolution_bitcast_fusion
  123.6 4.6 copy.51
  139.2 39.9 %while.35 = (s32[]{:T(128)}, bf16[2,1088,4,64]{1,3,2,0:T(8,128)(2,1)S(1)}, f32[2,4,1088]{2,1,0:T(4,128)S(1)}, bf16[2,1088,4,64]{1,3,2,0:T(8,128)(2,1)}, s32[2]{0...) while((s32[]{:T(128)}, ...), condition=%wide.region_7.8_spmd, body=%wide.region_2.7_spmd.sunk | while | flops 951075200 | bytes 50647132 | solution.py:161
  154.5 4.3 fusion.216
  174.1 4.3 fusion.216
  184.3 6.2 fusion.156
  191.2 150.5 %reduce-scatter.5.cloned.1.call-done = f32[544,1024]{1,0:T(8,128)} async-done(((f32[2176,1024]{1,0:T(8,128)}), f32[544,1024]{1,0:T(8,128)}) %reduce-scatter.5.cloned.1.call-update) | async-done | bytes 2228240 | tf_op jit(solution)/shard_map/reduce_scatter | solution.py:163
  349.5 86.3 %all-gather.7.cloned.1.call-done = bf16[2176,1024]{1,0:T(8,128)(2,1)} async-done(((bf16[544,1024]{1,0:T(8,128)(2,1)}), bf16[2176,1024]{1,0:T(8,128)(2,1)}) %all-gather.7.cloned.1.call-update) | async-done | bytes 4456464 | tf_op jit(solution)/shard_map/all_gather | solution.py:177
  435.8 11.9 multiply_convert_fusion.2
  449.8 7.0 fusion.157
  457.5 150.5 %reduce-scatter.7.cloned.1.call-done = f32[544,1024]{1,0:T(8,128)} async-done(((f32[2176,1024]{1,0:T(8,128)}), f32[544,1024]{1,0:T(8,128)}) %reduce-scatter.7.cloned.1.call-update) | async-done | bytes 2228240 | tf_op jit(solution)/shard_map/reduce_scatter | solution.py:183
  615.6 86.3 %all-gather.9.cloned.1.call-done = bf16[2176,1024]{1,0:T(8,128)(2,1)} async-done(((bf16[544,1024]{1,0:T(8,128)(2,1)}), bf16[2176,1024]{1,0:T(8,128)(2,1)}) %all-gather.9.cloned.1.call-update) | async-done | bytes 4456464 | tf_op jit(solution)/shard_map/all_gather | solution.py:199
  701.9 15.1 convert_reduce_fusion
  719.0 7.2 fusion.158
  726.7 150.8 %reduce-scatter.9.cloned.1.call-done = f32[544,1024]{1,0:T(8,128)} async-done(((f32[2176,1024]{1,0:T(8,128)}), f32[544,1024]{1,0:T(8,128)}) %reduce-scatter.9.cloned.1.call-update) | async-done | bytes 2228240 | tf_op jit(solution)/shard_map/reduce_scatter | solution.py:206
  881.5 5.1 multiply_reduce_fusion.3
  889.1 9.7 fusion.161
  898.9 9.3 fusion.160
  908.1 67.3 %all-gather.11.cloned.1.call-done = bf16[2176,1024]{1,0:T(8,128)(2,1)} async-done(((bf16[544,1024]{1,0:T(8,128)(2,1)}), bf16[2176,1024]{1,0:T(8,128)(2,1)}) %all-gather.11.cloned.1.call-update) | async-done | bytes 4456464 | tf_op jit(solution)/shard_map/all_gather | solution.py:221
  987.1 199.1 %while.36 = (s32[]{:T(128)}, f32[2,1088,4,64]{1,0,3,2:T(2,128)}, bf16[2,1088,4,64]{1,3,2,0:T(8,128)(2,1)}, bf16[2,1088,4,64]{1,3,2,0:T(8,128)(2,1)}, bf16[2,1088...) while((s32[]{:T(128)}, f32[2,1088,4,64]{1,0,3,2:T(2,128)}, ...), condition=%wide.region_26.27_spmd, body=%wide.region_23.26_spmd.sunk | while | flops 2328682240 | bytes 256355056 | solution.py:228
  995.1 4.4 fusion.236
  999.5 9.9 fusion.238
  1009.4 9.1 fusion.237
  1018.5 4.9 exponential_select_fusion.4
  1028.3 6.5 fusion.233
  1034.8 15.7 fusion.239
  1050.5 15.0 fusion.234
  1066.9 19.6 %dynamic_update_slice.42 = f32[2,1088,4,64]{1,0,3,2:T(2,128)} dynamic-update-slice(f32[2,1088,4,64]{1,0,3,2:T(2,128)} %get-tuple-element.608, f32[1,1088,4,64]{1,0,3,2:T(1,128)S(1)} %copy.111, s32[]{:T(128)S(6)} %copy.130, s32[]{:T(128)} %constant.238.clone.1..sunk.1, s32[]{:T(128)} %constant.238.clone.1..sunk.1, s32[]{:T(128)} %constant.238.clone.1..sunk.1) | dynamic-update-slice | bytes 2228228 | tf_op jit(solution)/shard_map/while/body/jit(dynamic_update_index_in_dim)/dynamic_update_slice | solution.py:161
  1094.5 4.4 fusion.236
  1098.9 9.9 fusion.238
  1108.8 9.1 fusion.237
  1117.8 4.9 exponential_select_fusion.4
  1127.7 6.5 fusion.233
  1134.2 15.8 fusion.239
  1149.9 14.9 fusion.234
  1166.3 19.6 %dynamic_update_slice.42 = f32[2,1088,4,64]{1,0,3,2:T(2,128)} dynamic-update-slice(f32[2,1088,4,64]{1,0,3,2:T(2,128)} %get-tuple-element.608, f32[1,1088,4,64]{1,0,3,2:T(1,128)S(1)} %copy.111, s32[]{:T(128)S(6)} %copy.130, s32[]{:T(128)} %constant.238.clone.1..sunk.1, s32[]{:T(128)} %constant.238.clone.1..sunk.1, s32[]{:T(128)} %constant.238.clone.1..sunk.1) | dynamic-update-slice | bytes 2228228 | tf_op jit(solution)/shard_map/while/body/jit(dynamic_update_index_in_dim)/dynamic_update_slice | solution.py:161
  1192.7 4.4 reshape.437
  1204.3 4.5 reshape.436
  1208.8 4.8 fusion.159
  1213.6 5.6 fusion.140
  1220.5 7.8 bitcast_convert_fusion
  1228.9 13.3 all-reduce.3
  1242.2 149.4 %all-reduce.10.cloned.1.call-done = (f32[3,1024,256]{1,2,0:T(8,128)}, f32[256,1024]{1,0:T(8,128)}, f32[1024,1024]{1,0:T(8,128)}, f32[1024,1024]{1,0:T(8,128)}) async-done(((f32[3,1024,256]{1,2,0:T(8,128)}, f32[256,1024]{1,0:T(8,128)}, f32[1024,1024]{1,0:T(8,128)}, f32[1024,1024]{1,0:T(8,128)}), (f32[3,1024,256]{1,2,0:T(8,128)}, f32[256,1024]{1,0:T(8,128)}, f32[1024,1024]{1,0:T(8,128)}, ...) | async-done | bytes 12582928 | tf_op jit(solution)/shard_map/psum | solution.py:266
  1395.1 80.2 %reduce-scatter.11.cloned.1.call-done = bf16[544,1024]{1,0:T(8,128)(2,1)} async-done(((bf16[2176,1024]{1,0:T(8,128)(2,1)}), bf16[544,1024]{1,0:T(8,128)(2,1)}) %reduce-scatter.11.cloned.1.call-update) | async-done | bytes 1114128 | tf_op jit(solution)/shard_map/reduce_scatter | solution.py:245
  1484.1 41.4 %all-reduce.2 = (f32[1024]{0:T(1024)}, f32[1024]{0:T(1024)}, f32[4,1024]{1,0:T(4,128)}, f32[4,1024]{1,0:T(4,128)}) all-reduce(f32[1024]{0:T(1024)S(1)} %copy-done.42, f32[1024]{0:T(1024)S(1)} %copy-done.41, f32[4,1024]{1,0:T(4,128)S(1)} %pad_maximum_fusion.3, ...), channel_id=1, replica_groups=mesh['dp'=8,'mp'=4] {'dp','mp'}, use_global_device_ids=true, to_apply=%region_36.37 | all-reduce | flops 10240 | bytes 81920 | tf_op jit(solution)/shard_map/psum | solution.py:269
  1525.4 78.4 %all-reduce.8.cloned.1.call-done = f32[16,1024]{1,0:T(8,128)} async-done(((f32[16,1024]{1,0:T(8,128)}), f32[16,1024]{1,0:T(8,128)}) %all-reduce.8.cloned.1.call-update) | async-done | bytes 65552 | tf_op jit(solution)/shard_map/psum | solution.py:269
  1604.8 4.9 copy.144
  (292 shorter events, 168.7 us)
Async XLA Ops:
  7.2 428.6 %copy-start = (bf16[1024,1024]{1,0:T(8,128)(2,1)S(1)}, bf16[1024,1024]{1,0:T(8,128)(2,1)}, u32[]{:S(2)}) copy-start(bf16[1024,1024]{1,0:T(8,128)(2,1)} %param.38) | copy-start | bytes 6291460
  7.2 95.1 %all-gather.5.cloned.1.call-start = ((), (), s32[]{:S(2)}) async-start(), calls=%async_computation.4 | async-start | bytes 5570560 | tf_op jit(solution)/shard_map/all_gather | solution.py:149
  8.7 3.8 copy-start.34
  14.9 326.8 %reduce-scatter.5.cloned.1.call-start = ((), (), s32[]{:S(2)}) async-start(), calls=%async_computation.5 | async-start | bytes 11141120 | tf_op jit(solution)/shard_map/reduce_scatter | solution.py:163
  184.3 6.2 copy-start.19
  190.5 245.3 %all-gather.7.cloned.1.call-start = ((), (), s32[]{:S(2)}) async-start(), calls=%async_computation.6 | async-start | bytes 5570560 | tf_op jit(solution)/shard_map/all_gather | solution.py:177
  191.2 154.6 %copy-start.36 = (f32[1,1024]{1,0:T(1,128)S(1)}, f32[1,1024]{1,0:T(1,128)}, u32[]{:S(2)}) copy-start(f32[1,1024]{1,0:T(1,128)} %get-tuple-element.433) | copy-start | bytes 12292
  191.2 154.6 %copy-start.51 = (f32[1,1024]{1,0:T(1,128)S(1)}, f32[1,1024]{1,0:T(1,128)}, u32[]{:S(2)}) copy-start(f32[1,1024]{1,0:T(1,128)} %get-tuple-element.437) | copy-start | bytes 12292
  341.7 4.1 copy-start.5
  341.7 4.1 copy-start.9
  349.4 258.6 %reduce-scatter.7.cloned.1.call-start = ((), (), s32[]{:S(2)}) async-start(), calls=%async_computation.7 | async-start | bytes 11141120 | tf_op jit(solution)/shard_map/reduce_scatter | solution.py:183
  435.8 14.0 copy-start.58
  456.9 245.0 %all-gather.9.cloned.1.call-start = ((), (), s32[]{:S(2)}) async-start(), calls=%async_computation.8 | async-start | bytes 5570560 | tf_op jit(solution)/shard_map/all_gather | solution.py:199
  457.5 153.3 %copy-start.39 = (f32[1,1024]{1,0:T(1,128)S(1)}, f32[1,1024]{1,0:T(1,128)}, u32[]{:S(2)}) copy-start(f32[1,1024]{1,0:T(1,128)} %get-tuple-element.431) | copy-start | bytes 12292
  608.1 2.8 copy-start.16
  615.5 261.9 %reduce-scatter.9.cloned.1.call-start = ((), (), s32[]{:S(2)}) async-start(), calls=%async_computation.9 | async-start | bytes 11141120 | tf_op jit(solution)/shard_map/reduce_scatter | solution.py:206
  726.3 249.2 %all-gather.11.cloned.1.call-start = ((), (), s32[]{:S(2)}) async-start(), calls=%async_computation.10 | async-start | bytes 5570560 | tf_op jit(solution)/shard_map/all_gather | solution.py:221
  877.5 4.0 copy-start.18
  881.5 5.2 copy-start.10
  886.6 2.4 copy-start.12
  886.6 12.2 slice-start
  889.1 502.5 %all-reduce.10.cloned.1.call-start = ((), (), s32[]{:S(2)}) async-start(), calls=%async_computation.13 | async-start | bytes 25165824 | tf_op jit(solution)/shard_map/psum | solution.py:266
  889.1 9.7 slice-start.1
  898.9 76.6 %copy-start.29 = (bf16[256,1024]{1,0:T(8,128)(2,1)S(1)}, bf16[256,1024]{1,0:T(8,128)(2,1)}, u32[]{:S(2)}) copy-start(bf16[256,1024]{1,0:T(8,128)(2,1)} %param.36) | copy-start | bytes 1572868
  1018.5 5.0 copy-start.13
  1023.5 3.8 copy-start.2
  1028.3 6.5 copy-start.62
  1117.8 5.0 copy-start.13
  1122.8 3.8 copy-start.2
  1127.7 6.5 copy-start.62
  1186.2 3.4 copy-start.15
  1198.7 2.5 copy-start.21
  1204.3 4.5 copy-start.20
  1208.7 4.8 copy-start.24
  1208.8 4.8 copy-start.26
  1208.8 4.8 copy-start.27
  1208.8 4.8 copy-start.57
  1219.2 256.1 %reduce-scatter.11.cloned.1.call-start = ((), (), s32[]{:S(2)}) async-start(), calls=%async_computation.11 | async-start | bytes 5570560 | tf_op jit(solution)/shard_map/reduce_scatter | solution.py:245
  1228.3 375.6 %all-reduce.8.cloned.1.call-start = ((), (), s32[]{:S(2)}) async-start(), calls=%async_computation.12 | async-start | bytes 131072 | tf_op jit(solution)/shard_map/psum | solution.py:269
  1391.6 83.7 %copy-start.31 = (f32[544]{0:T(1024)S(1)}, f32[544]{0:T(1024)}, u32[]{:S(2)}) copy-start(f32[544]{0:T(1024)} %copy-done.30) | copy-start | bytes 6532
  1391.6 83.7 %copy-start.33 = (f32[544]{0:T(1024)S(1)}, f32[544]{0:T(1024)}, u32[]{:S(2)}) copy-start(f32[544]{0:T(1024)} %copy-done.32) | copy-start | bytes 6532
  1391.6 83.7 %copy-start.35 = (f32[1,1024]{1,0:T(1,128)S(1)}, f32[1,1024]{1,0:T(1,128)}, u32[]{:S(2)}) copy-start(f32[1,1024]{1,0:T(1,128)} %copy-done.34) | copy-start | bytes 12292
  1475.3 3.2 copy-start.6
  1475.3 3.2 copy-start.22
  1478.5 3.8 copy-start.40
  1482.4 121.5 %copy-start.28 = (f32[256,1024]{1,0:T(8,128)S(1)}, f32[256,1024]{1,0:T(8,128)}, u32[]{:S(2)}) copy-start(f32[256,1024]{1,0:T(8,128)} %get-tuple-element.637) | copy-start | bytes 3145732
  1604.8 4.9 copy-start.23
  1604.8 7.6 copy-start.1
  (32 other events, 49.1 us)
Sparse Core Ops, SparseCore 0:
  15.0 87.1 all-gather.4
  190.6 151.0 reduce-scatter.4
  349.5 86.1 all-gather.6
  457.0 151.0 reduce-scatter.6
  615.6 86.1 all-gather.8
  726.4 151.0 reduce-scatter.8
  889.2 86.1 all-gather.10
  1219.4 172.1 all-reduce.9
  1394.0 81.2 reduce-scatter.10
  1484.1 119.7 all-reduce.7
where the time goes:
time: 1630 us; the launch traced here: 1620 us
  waiting for transfers between devices  1090 us (67%)
  matrix products  263 us (16%)
  local copies, waits for them, and re-layouts  138 us (8%)
  other arithmetic  59.1 us (4%)
  blocking collectives  54.6 us (3%)
    reduce_scatter x1, waiting for transfers between devices, on_device(): lax.psum_scatter(jnp.dot(lax.slice_in_dim(grad_pre_low, 0, row_count * la...  151 us
    reduce_scatter x1, waiting for transfers between devices, on_device(): lax.psum_scatter(jnp.dot(lax.slice_in_dim(activated_low, 0, row_count * l...  151 us
    reduce_scatter x1, waiting for transfers between devices, on_device(): lax.psum_scatter(jnp.dot(lax.slice_in_dim(attended_low, 0, row_count * la...  151 us
    psum x1, waiting for transfers between devices, on_device(): lax.psum((qkv_grad, qv_bias_grad, out_grad, up_grad, up_bias_grad, down_g...  149 us
    all_gather x1, waiting for transfers between devices, on_device(): normed_all = lax.all_gather(normed_low, 'mp', axis=0, tiled=True)  87.1 us
    all_gather x1, waiting for transfers between devices, on_device(): grad_ffn_all = lax.all_gather(grad_ffn_low, 'mp', axis=0, tiled=True)  86.3 us
    all_gather x1, waiting for transfers between devices, on_device(): mid_all = lax.all_gather(mid_low, 'mp', axis=0, tiled=True)  86.3 us
    reduce_scatter x1, waiting for transfers between devices, on_device(): lax.psum_scatter(jnp.einsum('cte,cde->td', lax.slice_in_dim(grad_projecte...  80.2 us
  transfers between devices with their start and end apart: 10, of which 10 were waited for; matrix products, arithmetic and copies ran while one was open for 2% of the time, Pallas kernels for 0%

commit v1 on v0

--- a/solution.py
+++ b/solution.py
@@ -267,7 +267,7 @@
         (qkv_grad, qv_bias_grad, out_grad, up_grad, up_bias_grad, down_grad), "dp"
     )
     gain_grad, shift_grad, out_bias_grad, down_bias_grad, table_grad = lax.psum(
-        (gain_parts, shift_parts, out_bias_part, down_bias_part, table_part), ("dp", "mp")
+        lax.psum((gain_parts, shift_parts, out_bias_part, down_bias_part, table_part), "mp"), "dp"
     )
     return (
         output,

time: 1630 us -> 1550 us (0.951)
  waiting for transfers between devices: 1090 us -> 1020 us
    psum x1, waiting for transfers between devices: 78.4 us -> 28 us  [on_device(): lax.psum((gain_parts, shift_parts, out_bias_part, down_bias_part, table_p...]
    psum x1, blocking collectives: 41.4 us -> 14.9 us  [on_device(): lax.psum((gain_parts, shift_parts, out_bias_part, down_bias_part, table_p...]
    reduce_scatter x1, waiting for transfers between devices: 80.2 us -> 54.3 us  [on_device(): lax.psum_scatter(jnp.einsum('cte,cde->td', lax.slice_in_dim(grad_projecte...]
    all_gather x1, waiting for transfers between devices: 67.3 us -> 86.3 us  [on_device(): grad_branch_all = lax.all_gather(grad_branch_low, 'mp', axis=0, tiled=True)]
where the time goes in v1:
time: 1550 us; the launch traced here: 1540 us
  waiting for transfers between devices  1020 us (66%)
  matrix products  264 us (17%)
  local copies, waits for them, and re-layouts  137 us (9%)
  other arithmetic  59.1 us (4%)
  blocking collectives  44.4 us (3%)
    reduce_scatter x1, waiting for transfers between devices, on_device(): lax.psum_scatter(jnp.dot(lax.slice_in_dim(grad_pre_low, 0, row_count * la...  151 us
    reduce_scatter x1, waiting for transfers between devices, on_device(): lax.psum_scatter(jnp.dot(lax.slice_in_dim(activated_low, 0, row_count * l...  151 us
    reduce_scatter x1, waiting for transfers between devices, on_device(): lax.psum_scatter(jnp.dot(lax.slice_in_dim(attended_low, 0, row_count * la...  151 us
    psum x1, waiting for transfers between devices, on_device(): lax.psum((qkv_grad, qv_bias_grad, out_grad, up_grad, up_bias_grad, down_g...  139 us
    all_gather x1, waiting for transfers between devices, on_device(): normed_all = lax.all_gather(normed_low, 'mp', axis=0, tiled=True)  87.1 us
    all_gather x1, waiting for transfers between devices, on_device(): grad_ffn_all = lax.all_gather(grad_ffn_low, 'mp', axis=0, tiled=True)  86.3 us
    all_gather x1, waiting for transfers between devices, on_device(): grad_branch_all = lax.all_gather(grad_branch_low, 'mp', axis=0, tiled=True)  86.3 us
    all_gather x1, waiting for transfers between devices, on_device(): mid_all = lax.all_gather(mid_low, 'mp', axis=0, tiled=True)  86.3 us
  transfers between devices with their start and end apart: 10, of which 10 were waited for; matrix products, arithmetic and copies ran while one was open for 2% of the time, Pallas kernels for 0%

profile of v1, /device:TPU:1, one launch (start us, length us, event | category | flops | bytes accessed | tf_op | source)
XLA Modules:
  0.0 1540.4 jit_solution(2936672181389591621)
XLA Ops:
  15.2 87.1 %all-gather.5.cloned.1.call-done = bf16[2176,1024]{1,0:T(8,128)(2,1)} async-done(((bf16[544,1024]{1,0:T(8,128)(2,1)}), bf16[2176,1024]{1,0:T(8,128)(2,1)}) %all-gather.5.cloned.1.call-update) | async-done | bytes 4456464 | tf_op jit(solution)/shard_map/all_gather | solution.py:149
  102.3 5.9 convolution_bitcast_fusion
  123.6 4.6 copy.51
  139.1 39.8 %while.35 = (s32[]{:T(128)}, bf16[2,1088,4,64]{1,3,2,0:T(8,128)(2,1)S(1)}, f32[2,4,1088]{2,1,0:T(4,128)S(1)}, bf16[2,1088,4,64]{1,3,2,0:T(8,128)(2,1)}, s32[2]{0...) while((s32[]{:T(128)}, ...), condition=%wide.region_7.8_spmd, body=%wide.region_2.7_spmd.sunk | while | flops 951075200 | bytes 50647132 | solution.py:161
  154.3 4.3 fusion.216
  173.9 4.3 fusion.216
  184.1 6.2 fusion.156
  191.0 150.5 %reduce-scatter.5.cloned.1.call-done = f32[544,1024]{1,0:T(8,128)} async-done(((f32[2176,1024]{1,0:T(8,128)}), f32[544,1024]{1,0:T(8,128)}) %reduce-scatter.5.cloned.1.call-update) | async-done | bytes 2228240 | tf_op jit(solution)/shard_map/reduce_scatter | solution.py:163
  349.3 86.3 %all-gather.7.cloned.1.call-done = bf16[2176,1024]{1,0:T(8,128)(2,1)} async-done(((bf16[544,1024]{1,0:T(8,128)(2,1)}), bf16[2176,1024]{1,0:T(8,128)(2,1)}) %all-gather.7.cloned.1.call-update) | async-done | bytes 4456464 | tf_op jit(solution)/shard_map/all_gather | solution.py:177
  435.6 11.9 multiply_convert_fusion.2
  449.5 7.0 fusion.157
  457.2 150.6 %reduce-scatter.7.cloned.1.call-done = f32[544,1024]{1,0:T(8,128)} async-done(((f32[2176,1024]{1,0:T(8,128)}), f32[544,1024]{1,0:T(8,128)}) %reduce-scatter.7.cloned.1.call-update) | async-done | bytes 2228240 | tf_op jit(solution)/shard_map/reduce_scatter | solution.py:183
  615.3 86.3 %all-gather.9.cloned.1.call-done = bf16[2176,1024]{1,0:T(8,128)(2,1)} async-done(((bf16[544,1024]{1,0:T(8,128)(2,1)}), bf16[2176,1024]{1,0:T(8,128)(2,1)}) %all-gather.9.cloned.1.call-update) | async-done | bytes 4456464 | tf_op jit(solution)/shard_map/all_gather | solution.py:199
  701.6 15.1 convert_reduce_fusion
  718.7 7.2 fusion.158
  726.0 151.2 %reduce-scatter.9.cloned.1.call-done = f32[544,1024]{1,0:T(8,128)} async-done(((f32[2176,1024]{1,0:T(8,128)}), f32[544,1024]{1,0:T(8,128)}) %reduce-scatter.9.cloned.1.call-update) | async-done | bytes 2228240 | tf_op jit(solution)/shard_map/reduce_scatter | solution.py:206
  881.2 5.1 multiply_reduce_fusion.3
  888.8 86.3 %all-gather.11.cloned.1.call-done = bf16[2176,1024]{1,0:T(8,128)(2,1)} async-done(((bf16[544,1024]{1,0:T(8,128)(2,1)}), bf16[2176,1024]{1,0:T(8,128)(2,1)}) %all-gather.11.cloned.1.call-update) | async-done | bytes 4456464 | tf_op jit(solution)/shard_map/all_gather | solution.py:221
  986.7 199.2 %while.36 = (s32[]{:T(128)}, f32[2,1088,4,64]{1,0,3,2:T(2,128)}, bf16[2,1088,4,64]{1,3,2,0:T(8,128)(2,1)}, bf16[2,1088,4,64]{1,3,2,0:T(8,128)(2,1)}, bf16[2,1088...) while((s32[]{:T(128)}, f32[2,1088,4,64]{1,0,3,2:T(2,128)}, ...), condition=%wide.region_26.27_spmd, body=%wide.region_23.26_spmd.sunk | while | flops 2328682240 | bytes 256355056 | solution.py:228
  995.0 4.4 fusion.236
  999.4 9.9 fusion.238
  1009.3 9.0 fusion.237
  1018.3 4.9 exponential_select_fusion.4
  1028.2 6.5 fusion.233
  1034.7 15.7 %fusion.239 = bf16[2,1088,4,64]{1,3,2,0:T(8,128)(2,1)} fusion(bf16[2,1088,4,64]{1,3,2,0:T(8,128)(2,1)} %get-tuple-element.614, s32[]{:T(128)S(6)} %copy.130, f32[4,544,1088]{2,1,0:T(8,128)} %copy-done.2, f32[4,544,1088]{2,1,0:T(8,128)} %fusion.233, f32[544,4,64]{0,2,1:T(8,128)S(1)} %copy-done.60, bf16[2,1088,4,64]{1,3,2,0:T(8,128)(2,1)} %get-tuple-element.631, ...), kind=kOutput, calls=%fused_computation.66.clone.1 | convolution fusion | flops 315157696 | bytes 42108416 | tf_op jit(solution)/shard_map/while/body/eval_jaxpr/hqk,qhd->khd/dot_general | solution.py:111
  1050.4 14.9 fusion.234
  1066.8 19.6 %dynamic_update_slice.42 = f32[2,1088,4,64]{1,0,3,2:T(2,128)} dynamic-update-slice(f32[2,1088,4,64]{1,0,3,2:T(2,128)} %get-tuple-element.613, f32[1,1088,4,64]{1,0,3,2:T(1,128)S(1)} %copy.111, s32[]{:T(128)S(6)} %copy.130, s32[]{:T(128)} %constant.238.clone.1..sunk.1, s32[]{:T(128)} %constant.238.clone.1..sunk.1, s32[]{:T(128)} %constant.238.clone.1..sunk.1) | dynamic-update-slice | bytes 2228228 | tf_op jit(solution)/shard_map/while/body/jit(dynamic_update_index_in_dim)/dynamic_update_slice | solution.py:161
  1094.4 4.4 fusion.236
  1098.7 9.9 fusion.238
  1108.7 9.0 fusion.237
  1117.7 4.9 exponential_select_fusion.4
  1127.6 6.5 fusion.233
  1134.1 15.7 %fusion.239 = bf16[2,1088,4,64]{1,3,2,0:T(8,128)(2,1)} fusion(bf16[2,1088,4,64]{1,3,2,0:T(8,128)(2,1)} %get-tuple-element.614, s32[]{:T(128)S(6)} %copy.130, f32[4,544,1088]{2,1,0:T(8,128)} %copy-done.2, f32[4,544,1088]{2,1,0:T(8,128)} %fusion.233, f32[544,4,64]{0,2,1:T(8,128)S(1)} %copy-done.60, bf16[2,1088,4,64]{1,3,2,0:T(8,128)(2,1)} %get-tuple-element.631, ...), kind=kOutput, calls=%fused_computation.66.clone.1 | convolution fusion | flops 315157696 | bytes 42108416 | tf_op jit(solution)/shard_map/while/body/eval_jaxpr/hqk,qhd->khd/dot_general | solution.py:111
  1149.8 15.0 fusion.234
  1166.2 19.6 %dynamic_update_slice.42 = f32[2,1088,4,64]{1,0,3,2:T(2,128)} dynamic-update-slice(f32[2,1088,4,64]{1,0,3,2:T(2,128)} %get-tuple-element.613, f32[1,1088,4,64]{1,0,3,2:T(1,128)S(1)} %copy.111, s32[]{:T(128)S(6)} %copy.130, s32[]{:T(128)} %constant.238.clone.1..sunk.1, s32[]{:T(128)} %constant.238.clone.1..sunk.1, s32[]{:T(128)} %constant.238.clone.1..sunk.1) | dynamic-update-slice | bytes 2228228 | tf_op jit(solution)/shard_map/while/body/jit(dynamic_update_index_in_dim)/dynamic_update_slice | solution.py:161
  1192.5 4.4 reshape.437
  1204.1 4.5 reshape.436
  1208.6 7.8 bitcast_convert_fusion
  1216.4 9.9 fusion.161
  1226.4 9.7 fusion.160
  1236.1 5.6 fusion.140
  1241.8 54.3 %reduce-scatter.11.cloned.1.call-done = bf16[544,1024]{1,0:T(8,128)(2,1)} async-done(((bf16[2176,1024]{1,0:T(8,128)(2,1)}), bf16[544,1024]{1,0:T(8,128)(2,1)}) %reduce-scatter.11.cloned.1.call-update) | async-done | bytes 1114128 | tf_op jit(solution)/shard_map/reduce_scatter | solution.py:245
  1304.7 4.6 fusion.159
  1309.3 28.0 %all-reduce.8.cloned.1.call-done = f32[16,1024]{1,0:T(8,128)} async-done(((f32[16,1024]{1,0:T(8,128)}), f32[16,1024]{1,0:T(8,128)}) %all-reduce.8.cloned.1.call-update) | async-done | bytes 65552 | tf_op jit(solution)/shard_map/psum | solution.py:270
  1338.1 14.9 all-reduce.4
  1353.0 29.5 %all-reduce.2 = (f32[2,256]{1,0:T(2,128)}, f32[1024]{0:T(1024)}, f32[1024]{0:T(1024)}, f32[1024]{0:T(1024)}, f32[4,1024]{1,0:T(4,128)}, /*index=5*/f32[4,1024]{1,0:T(4,128)}) all-reduce(f32[2,256]{1,0:T(2,128)S(1)} %pad_maximum_fusion.5, f32[1024]{0:T(1024)S(1)} %get-tuple-element.409, ...), channel_id=1, replica_groups=mesh['dp'=8,'mp'=4] {'dp'}, use_global_device_ids=true, to_apply=%region_33.34 | all-reduce | flops 11776 | bytes 94208 | tf_op jit(solution)/shard_map/psum | solution.py:266
  1382.5 138.6 %all-reduce.10.cloned.1.call-done = (f32[3,1024,256]{1,2,0:T(8,128)}, f32[256,1024]{1,0:T(8,128)}, f32[1024,1024]{1,0:T(8,128)}, f32[1024,1024]{1,0:T(8,128)}, f32[16,1024]{1,0:T(8,128)}) async-done(((f32[3,1024,256]{1,2,0:T(8,128)}, f32[256,1024]{1,0:T(8,128)}, f32[1024,1024]{1,0:T(8,128)}, f32[1024,1024]{1,0:T(8,128)}, f32[16,1024]{1,0:T(8,128)}), (f32[3,1024,256]{1,2,0:T(8,128)}, f32[256,1024]{1,0:T(8,128)}, ...) | async-done | bytes 12648464 | tf_op jit(solution)/shard_map/psum | solution.py:266
  1525.7 4.9 copy.145
  (288 shorter events, 167.1 us)
Async XLA Ops:
  7.2 428.4 %copy-start = (bf16[1024,1024]{1,0:T(8,128)(2,1)S(1)}, bf16[1024,1024]{1,0:T(8,128)(2,1)}, u32[]{:S(2)}) copy-start(bf16[1024,1024]{1,0:T(8,128)(2,1)} %param.38) | copy-start | bytes 6291460
  7.2 95.1 %all-gather.5.cloned.1.call-start = ((), (), s32[]{:S(2)}) async-start(), calls=%async_computation.4 | async-start | bytes 5570560 | tf_op jit(solution)/shard_map/all_gather | solution.py:149
  8.7 3.8 copy-start.33
  14.9 326.6 %reduce-scatter.5.cloned.1.call-start = ((), (), s32[]{:S(2)}) async-start(), calls=%async_computation.5 | async-start | bytes 11141120 | tf_op jit(solution)/shard_map/reduce_scatter | solution.py:163
  184.1 6.2 copy-start.19
  190.3 245.3 %all-gather.7.cloned.1.call-start = ((), (), s32[]{:S(2)}) async-start(), calls=%async_computation.6 | async-start | bytes 5570560 | tf_op jit(solution)/shard_map/all_gather | solution.py:177
  191.0 154.6 %copy-start.35 = (f32[1,1024]{1,0:T(1,128)S(1)}, f32[1,1024]{1,0:T(1,128)}, u32[]{:S(2)}) copy-start(f32[1,1024]{1,0:T(1,128)} %get-tuple-element.438) | copy-start | bytes 12292
  191.0 154.7 %copy-start.50 = (f32[1,1024]{1,0:T(1,128)S(1)}, f32[1,1024]{1,0:T(1,128)}, u32[]{:S(2)}) copy-start(f32[1,1024]{1,0:T(1,128)} %get-tuple-element.442) | copy-start | bytes 12292
  341.5 4.1 copy-start.5
  341.5 4.1 copy-start.9
  349.2 258.5 %reduce-scatter.7.cloned.1.call-start = ((), (), s32[]{:S(2)}) async-start(), calls=%async_computation.7 | async-start | bytes 11141120 | tf_op jit(solution)/shard_map/reduce_scatter | solution.py:183
  435.6 13.9 copy-start.56
  456.5 245.0 %all-gather.9.cloned.1.call-start = ((), (), s32[]{:S(2)}) async-start(), calls=%async_computation.8 | async-start | bytes 5570560 | tf_op jit(solution)/shard_map/all_gather | solution.py:199
  457.2 153.3 %copy-start.38 = (f32[1,1024]{1,0:T(1,128)S(1)}, f32[1,1024]{1,0:T(1,128)}, u32[]{:S(2)}) copy-start(f32[1,1024]{1,0:T(1,128)} %get-tuple-element.436) | copy-start | bytes 12292
  607.8 2.8 copy-start.16
  615.2 262.0 %reduce-scatter.9.cloned.1.call-start = ((), (), s32[]{:S(2)}) async-start(), calls=%async_computation.9 | async-start | bytes 11141120 | tf_op jit(solution)/shard_map/reduce_scatter | solution.py:206
  726.0 249.1 %all-gather.11.cloned.1.call-start = ((), (), s32[]{:S(2)}) async-start(), calls=%async_computation.10 | async-start | bytes 5570560 | tf_op jit(solution)/shard_map/all_gather | solution.py:221
  877.2 4.0 copy-start.18
  881.2 5.2 copy-start.10
  886.3 88.8 %copy-start.28 = (bf16[256,1024]{1,0:T(8,128)(2,1)S(1)}, bf16[256,1024]{1,0:T(8,128)(2,1)}, u32[]{:S(2)}) copy-start(bf16[256,1024]{1,0:T(8,128)(2,1)} %param.36) | copy-start | bytes 1572868
  888.7 407.3 %reduce-scatter.11.cloned.1.call-start = ((), (), s32[]{:S(2)}) async-start(), calls=%async_computation.11 | async-start | bytes 5570560 | tf_op jit(solution)/shard_map/reduce_scatter | solution.py:245
  992.6 2.4 copy-start.3
  1018.3 5.0 copy-start.13
  1023.3 3.8 copy-start.2
  1028.2 6.5 copy-start.60
  1091.9 2.4 copy-start.3
  1117.7 5.0 copy-start.13
  1122.7 3.8 copy-start.2
  1127.6 6.5 copy-start.60
  1186.0 3.4 copy-start.15
  1198.5 2.5 copy-start.21
  1204.1 4.5 copy-start.24
  1216.4 120.9 %all-reduce.8.cloned.1.call-start = ((), (), s32[]{:S(2)}) async-start(), calls=%async_computation.12 | async-start | bytes 131072 | tf_op jit(solution)/shard_map/psum | solution.py:270
  1216.4 19.6 %slice-start = ((s8[4456448]{0:T(1024)(128)(4,1)}), s8[4194304]{0:T(1024)(128)(4,1)S(1)}, s32[]{:S(2)}) async-start(s8[4456448]{0:T(1024)(128)(4,1)} %bitcast.261), calls=%async_computation.14 | async-start | bytes 8388608
  1226.4 9.7 copy-start.25
  1226.4 9.7 copy-start.26
  1226.4 9.7 slice-start.1
  1236.1 60.0 %copy-start.30 = (f32[544]{0:T(1024)S(1)}, f32[544]{0:T(1024)}, u32[]{:S(2)}) copy-start(f32[544]{0:T(1024)} %copy-done.29) | copy-start | bytes 6532
  1236.1 60.0 %copy-start.32 = (f32[544]{0:T(1024)S(1)}, f32[544]{0:T(1024)}, u32[]{:S(2)}) copy-start(f32[544]{0:T(1024)} %copy-done.31) | copy-start | bytes 6532
  1236.1 60.0 %copy-start.34 = (f32[1,1024]{1,0:T(1,128)S(1)}, f32[1,1024]{1,0:T(1,128)}, u32[]{:S(2)}) copy-start(f32[1,1024]{1,0:T(1,128)} %copy-done.33) | copy-start | bytes 12292
  1296.1 3.2 copy-start.6
  1296.1 3.2 copy-start.22
  1299.3 3.8 copy-start.39
  1304.6 216.5 %all-reduce.10.cloned.1.call-start = ((), (), s32[]{:S(2)}) async-start(), calls=%async_computation.13 | async-start | bytes 25296896 | tf_op jit(solution)/shard_map/psum | solution.py:266
  1337.3 15.7 %copy-start.51 = (f32[1024]{0:T(1024)S(1)}, f32[1024]{0:T(1024)}, u32[]{:S(2)}) copy-start(f32[1024]{0:T(1024)} %get-tuple-element.413) | copy-start | bytes 12292
  1521.1 3.6 copy-start.27
  1525.7 4.9 copy-start.23
  1525.7 7.6 copy-start.1
  (30 other events, 38.7 us)
Sparse Core Ops, SparseCore 0:
  15.0 87.2 all-gather.4
  190.4 151.0 reduce-scatter.4
  349.4 86.1 all-gather.6
  456.7 151.0 reduce-scatter.6
  615.3 86.1 all-gather.8
  726.1 151.0 reduce-scatter.8
  888.9 86.1 all-gather.10
  1216.5 79.5 reduce-scatter.10
  1304.8 32.4 all-reduce.7
  1343.3 177.8 all-reduce.9
